TPU v7x, 256 devices: a whole 4x4x8 slice. The times are simulated.
256 devices in a mesh: samp: 8 (over z), feat: 32 (over y, x, core).
Axes of the slice: x: 4, y: 4, z: 8, core: 2. Of those that a mesh axis runs over, the one named last changes fastest.
Arguments:
- data: bfloat16 [32768, 512], P('samp'), may hold values from -6 to 6
- omega: bfloat16 [512, 24576], P(None, 'feat'), may hold values from -0.25 to 0.25
- phase: float32 [24576], P('feat'), may hold values from -3.140625 to 3.140625
- earlier: bfloat16 [24576, 12288], P('feat', 'samp'), may hold values from -3 to 3, as said below
- ridge: float32 [1], replicated, may hold values from 0.5 to 2
Outputs:
- factor: float32 [24576, 512], P('feat')
Inputs may be any that keep to these rules, and one draw needn't show every extreme that they name: The spectral norm of earlier[:512] is at most 0.56, so that shifted[:512] is positive definite.
All inputs are finite; a program needn't handle non-finite values.
Results may differ from a plain program's by a relative error of at most 0.015.
Values may be sent and summed in bfloat16 or wider, within the bound.
No kernel may reach another device: no remote copies, remote signals or barrier semaphores. Data moves between devices by JAX's collectives and lax.ppermute only.
A program may use at most 128 MiB of HBM per device.

v0:
```python
import functools
import math

import jax
import jax.numpy as jnp
import numpy as np
from jax import lax
from jax.experimental import pallas as pl
from jax.experimental.pallas import tpu as pltpu
from jax.sharding import PartitionSpec as P


PANEL = 512
SIDE = 4
SAMPLE_BLOCK = 512
EXTRA = 16
HIGHEST = lax.Precision.HIGHEST
NT = (((1,), (1,)), ((), ()))
TN = (((0,), (0,)), ((), ()))
INV_TURN = 1.0 / (2.0 * math.pi)
DEGREE = 3


def sine_coefficients():
    u = np.cos(np.pi * (np.arange(4000) + 0.5) / 4000) * 0.25
    fit = np.polynomial.chebyshev.Chebyshev.fit(u * u, -np.sin(2 * np.pi * u) / u, DEGREE, domain=[0, 1 / 16])
    poly = fit.convert(kind=np.polynomial.Polynomial, domain=[-1, 1], window=[-1, 1])
    return [float(v) for v in poly.coef]


SINE = sine_coefficients()


def scaled_cos(turns, scale):
    r = turns - jnp.round(turns)
    u = jnp.abs(r) - 0.25
    s = u * u
    coefs = [v * scale for v in SINE]
    p = coefs[DEGREE]
    for v in coefs[DEGREE - 1::-1]:
        p = p * s + v
    return p * u


def column(line):
    n = line.shape[1]
    eye = lax.broadcasted_iota(jnp.int32, (128, 128), 0) == lax.broadcasted_iota(jnp.int32, (128, 128), 1)
    parts = []
    for q in range(n // 128):
        square = jnp.broadcast_to(line[:, 128 * q:128 * q + 128], (128, 128))
        parts.append(jnp.sum(jnp.where(eye, square, 0.0), axis=1, keepdims=True))
    return jnp.concatenate(parts, axis=0)


def local_kernel(w_ref, ph_ref, x_ref, *refs, scale):
    o_ref, col_ref = refs[-2:]

    @pl.when(pl.program_id(0) == 0)
    def _():
        col_ref[...] = column(ph_ref[...])

    for r in range(w_ref.shape[0] // 256):
        part = slice(256 * r, 256 * r + 256)
        proj = lax.dot_general(w_ref[part, :], x_ref[...], NT, preferred_element_type=jnp.float32)
        o_ref[part, :] = scaled_cos(proj * INV_TURN + col_ref[part, :], scale).astype(jnp.bfloat16)


def local_features(wt, turns, data, scale, first, blocks, bs, before=None):
    rows, din = wt.shape
    samples = data.shape[0]
    done = [] if before is None else [before]
    return pl.pallas_call(
        functools.partial(local_kernel, scale=scale),
        grid=(blocks,),
        in_specs=[
            pl.BlockSpec((rows, din), lambda i: (0, 0)),
            pl.BlockSpec((1, rows), lambda i: (0, 0)),
            pl.BlockSpec((bs, din), lambda i: (first + i, 0)),
            *[pl.BlockSpec(memory_space=pl.ANY) for _ in done],
        ],
        out_specs=pl.BlockSpec((rows, bs), lambda i: (0, first + i)),
        out_shape=jax.ShapeDtypeStruct((rows, samples), jnp.bfloat16),
        scratch_shapes=[pltpu.VMEM((rows, 1), jnp.float32)],
        input_output_aliases={3: 0} if done else {},
        cost_estimate=pl.CostEstimate(flops=2 * rows * blocks * bs * din, bytes_accessed=3 * blocks * bs * din, transcendentals=0),
        name="local_features",
    )(wt, turns, data, *done)


def place_of(feat):
    return lax.div(feat, 2 * SIDE), lax.rem(lax.div(feat, 2), SIDE), lax.rem(feat, 2)


def gram_kernel(feat_ref, *refs, scale, sub):
    slots, (x_ref, f_ref, e_ref, s_ref, d_ref, v_ref, acc_ref, ph_ref, panel_ref) = refs[:8], refs[8:]
    i = pl.program_id(0)
    rows = s_ref.shape[0]
    y, x, c = place_of(feat_ref[0])
    first = pl.multiple_of(feat_ref[0] * 16, 16)

    def sixteen(p):
        within = pl.ds(pl.multiple_of(lax.rem(first, 256), 16), 16)
        return v_ref[p + lax.div(first, 256), within, :]

    def add(cols, left, right, sign):
        out = lax.dot_general(left, right, NT, preferred_element_type=jnp.float32)
        s_ref[:, cols] += sign * out[:rows]
        acc_ref[:, cols] += sign * out[rows:]

    @pl.when(i == 0)
    def _():
        for k in range(SIDE):
            along_x = lax.rem(x - k + SIDE, SIDE)
            along_y = SIDE + lax.rem(y - k + SIDE, SIDE)
            v_ref[jnp.where(c == 0, along_x, along_y)] = slots[k][...]
            v_ref[jnp.where(c == 0, along_y, along_x)] = slots[SIDE + k][...]
        tail = v_ref[0, 256:256 + EXTRA, :].astype(jnp.float32)
        ph_ref[...] = column((tail[0:1] + tail[1:2]) + tail[2:3])
        s_ref[...] = jnp.zeros_like(s_ref)
        acc_ref[...] = jnp.zeros_like(acc_ref)

    for chunk in range(3):
        @pl.when(i == chunk)
        def _(chunk=chunk):
            left = jnp.concatenate([e_ref[...], sixteen(2 + 2 * chunk)], axis=0)
            for h in range(2):
                add(slice(256 * h, 256 * h + 256), left, v_ref[2 + 2 * chunk + h, :256, :], -1.0)

    for j in range(x_ref.shape[0] // sub):
        at = slice(j * sub, j * sub + sub)
        for h in range(2):
            half = slice(256 * h, 256 * h + 256)
            proj = lax.dot_general(v_ref[h, :256, :], x_ref[at, :], NT, preferred_element_type=jnp.float32)
            panel_ref[j, half, :] = scaled_cos(proj * INV_TURN + ph_ref[half, :], scale).astype(jnp.bfloat16)
        mine = panel_ref[j, pl.ds(first, 16), :]
        left = jnp.concatenate([f_ref[:, at], mine], axis=0)
        for h in range(2):
            half = slice(256 * h, 256 * h + 256)
            add(half, left, panel_ref[j, half, :], 1.0)

    @pl.when(i == pl.num_programs(0) - 1)
    def _():
        for k in range(d_ref.shape[0]):
            d_ref[k] = acc_ref[...]


def gram(feat, slots, data, local, earlier, scale, copies, bs=1024, sub=512):
    rows = earlier.shape[0]
    samples, din = data.shape
    return pl.pallas_call(
        functools.partial(gram_kernel, scale=scale, sub=sub),
        grid=(samples // bs,),
        in_specs=[
            pl.BlockSpec(memory_space=pltpu.SMEM),
            *[pl.BlockSpec(memory_space=pltpu.VMEM) for _ in slots],
            pl.BlockSpec((bs, din), lambda i: (i, 0)),
            pl.BlockSpec((rows, bs), lambda i: (0, i)),
            pl.BlockSpec((rows, PANEL), lambda i: (0, jnp.minimum(i, 2))),
        ],
        out_specs=[
            pl.BlockSpec((rows, PANEL), lambda i: (0, 0)),
            pl.BlockSpec((copies, 16, PANEL), lambda i: (0, 0, 0)),
        ],
        out_shape=[
            jax.ShapeDtypeStruct((rows, PANEL), jnp.float32),
            jax.ShapeDtypeStruct((copies, 16, PANEL), jnp.float32),
        ],
        scratch_shapes=[
            pltpu.VMEM((2 * SIDE, *slots[0].shape), jnp.bfloat16),
            pltpu.VMEM((16, PANEL), jnp.float32),
            pltpu.VMEM((PANEL, 1), jnp.float32),
            pltpu.VMEM((bs // sub, PANEL, sub), jnp.bfloat16),
        ],
        cost_estimate=pl.CostEstimate(flops=8 << 30, bytes_accessed=16 << 20, transcendentals=0),
        compiler_params=pltpu.CompilerParams(vmem_limit_bytes=50 << 20),
        name="gram",
    )(feat, *slots, data, local, earlier)


def split2(v):
    high = v.astype(jnp.bfloat16)
    return high, (v - high.astype(jnp.float32)).astype(jnp.bfloat16)


def split3(v):
    high = v.astype(jnp.bfloat16)
    rest = v - high.astype(jnp.float32)
    mid = rest.astype(jnp.bfloat16)
    return high, mid, (rest - mid.astype(jnp.float32)).astype(jnp.bfloat16)


def spread(block, j):
    return jnp.broadcast_to(block[:, j:j + 1], (8, 128))


def block_inverse(n_ref, lb_ref):
    sub = lax.broadcasted_iota(jnp.int32, (8, 128), 0)
    lane = lax.broadcasted_iota(jnp.int32, (8, 128), 1)

    def step(s, carry):
        rows0, rows1, left, right = carry
        k = pl.multiple_of(s * 8, 8)
        shift = jnp.where(s == 0, 0, 128 - k)
        n_ref[...] -= lax.dot_general(left, right, TN, preferred_element_type=jnp.float32)
        pivot = pltpu.roll(rows0, shift, 1)
        a = [[None] * 8 for _ in range(8)]
        for j in range(8):
            col = spread(pivot, j)
            for i in range(j, 8):
                a[i][j] = jnp.broadcast_to(col[i:i + 1, :], (8, 128))
        low = [[None] * 8 for _ in range(8)]
        root = []
        for j in range(8):
            inverse = 1.0 / a[j][j]
            root.append(lax.rsqrt(a[j][j]))
            for i in range(j + 1, 8):
                low[i][j] = a[i][j] * inverse
            for i in range(j + 1, 8):
                for m in range(j + 1, i + 1):
                    a[i][m] = a[i][m] - low[i][j] * a[m][j]
        t = [[None] * 8 for _ in range(8)]
        for j in range(8):
            t[j][j] = root[j]
            for i in range(j + 1, 8):
                acc = low[i][j]
                for m in range(j + 1, i):
                    acc = acc + low[i][m] * t[m][j]
                t[i][j] = -acc
        for j in range(8):
            for i in range(j + 1, 8):
                t[i][j] = root[i] * t[i][j]
        w0 = jnp.zeros((8, 128), jnp.float32)
        w1 = jnp.zeros((8, 128), jnp.float32)
        for j in range(8):
            col = jnp.where(sub == j, t[j][j], 0.0)
            for i in range(j + 1, 8):
                col = jnp.where(sub == i, t[i][j], col)
            w0 = w0 + col * jnp.broadcast_to(rows0[j:j + 1, :], (8, 128))
            w1 = w1 + col * jnp.broadcast_to(rows1[j:j + 1, :], (8, 128))
        lb_ref[pl.ds(k, 8), :] = w1
        after = jnp.minimum(k + 8, 120)
        after = pl.multiple_of(after, 8)
        next0 = n_ref[pl.ds(after, 8), :128]
        next1 = n_ref[pl.ds(after, 8), 128:]
        cross = pltpu.roll(next0, shift, 1)
        cols = [spread(cross, m) for m in range(8)]
        for j in range(8):
            factor = t[j][0] * cols[0]
            for m in range(1, j + 1):
                factor = factor + t[j][m] * cols[m]
            next0 = next0 - factor * jnp.broadcast_to(w0[j:j + 1, :], (8, 128))
            next1 = next1 - factor * jnp.broadcast_to(w1[j:j + 1, :], (8, 128))
        gh, gm, gl = split3(jnp.where(lane >= k + 8, w0, 0.0))
        wh, wm, wl = split3(jnp.concatenate([w0, w1], axis=1))
        left = jnp.concatenate([gh, gh, gm, gh, gm, gl], axis=0)
        right = jnp.concatenate([wh, wm, wh, wl, wm, wh], axis=0)
        return next0, next1, left, right

    start = (
        n_ref[:8, :128],
        n_ref[:8, 128:],
        jnp.zeros((48, 128), jnp.bfloat16),
        jnp.zeros((48, 256), jnp.bfloat16),
    )
    lax.fori_loop(0, 16, step, start)


def factor_kernel(ridge_ref, d_ref, high_ref, low_ref, m_ref, j_ref, n_ref, lb_ref):
    n = PANEL
    eye = lax.broadcasted_iota(jnp.int32, (n, n), 0) == lax.broadcasted_iota(jnp.int32, (n, n), 1)
    m_ref[...] = d_ref[...].reshape(n, n) + jnp.where(eye, ridge_ref[0], 0.0)
    j_ref[...] = jnp.where(eye, 1.0, 0.0)
    high_ref[...] = jnp.zeros((n, n), jnp.bfloat16)
    low_ref[...] = jnp.zeros((n, n), jnp.bfloat16)
    small = lax.broadcasted_iota(jnp.int32, (128, 128), 0) == lax.broadcasted_iota(jnp.int32, (128, 128), 1)
    for b in range(n // 128):
        r0, r1 = 128 * b, 128 * b + 128
        n_ref[:, :128] = m_ref[r0:r1, r0:r1]
        n_ref[:, 128:] = jnp.where(small, 1.0, 0.0)
        block_inverse(n_ref, lb_ref)
        lb = lb_ref[...]
        jb = jnp.dot(lb, j_ref[r0:r1, :r1], precision=HIGHEST, preferred_element_type=jnp.float32)
        high_ref[r0:r1, :r1], low_ref[r0:r1, :r1] = split2(jb)
        if r1 < n:
            r = jnp.dot(lb, m_ref[r0:r1, r1:], precision=HIGHEST, preferred_element_type=jnp.float32)
            m_ref[r1:, r1:] -= lax.dot_general(r, r, TN, precision=HIGHEST, preferred_element_type=jnp.float32)
            j_ref[r1:, :r1] -= lax.dot_general(r, jb, TN, precision=HIGHEST, preferred_element_type=jnp.float32)


def factor_inverse(ridge, d):
    n = PANEL
    return pl.pallas_call(
        factor_kernel,
        out_shape=[jax.ShapeDtypeStruct((n, n), jnp.bfloat16)] * 2,
        in_specs=[pl.BlockSpec(memory_space=pltpu.SMEM), pl.BlockSpec(memory_space=pltpu.VMEM)],
        out_specs=[pl.BlockSpec(memory_space=pltpu.VMEM)] * 2,
        scratch_shapes=[
            pltpu.VMEM((n, n), jnp.float32),
            pltpu.VMEM((n, n), jnp.float32),
            pltpu.VMEM((128, 256), jnp.float32),
            pltpu.VMEM((128, 128), jnp.float32),
        ],
        cost_estimate=pl.CostEstimate(flops=8 << 30, bytes_accessed=2 << 20, transcendentals=0),
        compiler_params=pltpu.CompilerParams(vmem_limit_bytes=12 << 20),
        name="factor_inverse",
    )(ridge, d)


def solve_kernel(feat_ref, ridge_ref, s_ref, high_ref, low_ref, o_ref, *, rows):
    bs = s_ref.shape[0]
    row_ids = feat_ref[0] * rows + pl.program_id(0) * bs + lax.broadcasted_iota(jnp.int32, (bs, PANEL), 0)
    hit = row_ids == lax.broadcasted_iota(jnp.int32, (bs, PANEL), 1)
    sh, sl = split2(s_ref[...] + jnp.where(hit, ridge_ref[0], 0.0))
    for b in range(PANEL // 256):
        r0, r1 = 256 * b, 256 * b + 256
        out = lax.dot_general(sh[:, :r1], low_ref[r0:r1, :r1], NT, preferred_element_type=jnp.float32)
        out += lax.dot_general(sl[:, :r1], high_ref[r0:r1, :r1], NT, preferred_element_type=jnp.float32)
        o_ref[:, r0:r1] = out + lax.dot_general(sh[:, :r1], high_ref[r0:r1, :r1], NT, preferred_element_type=jnp.float32)


def solve(feat, ridge, s, high, low, bs=384):
    rows = s.shape[0]
    smem = pl.BlockSpec(memory_space=pltpu.SMEM)
    return pl.pallas_call(
        functools.partial(solve_kernel, rows=rows),
        grid=(rows // bs,),
        out_shape=jax.ShapeDtypeStruct(s.shape, jnp.float32),
        in_specs=[smem, smem, pl.BlockSpec((bs, PANEL), lambda i: (i, 0)), *[pl.BlockSpec(memory_space=pltpu.VMEM)] * 2],
        out_specs=pl.BlockSpec((bs, PANEL), lambda i: (i, 0)),
        cost_estimate=pl.CostEstimate(flops=6 * rows * PANEL * PANEL, bytes_accessed=4 << 20, transcendentals=0),
        compiler_params=pltpu.CompilerParams(vmem_limit_bytes=65_600_000),
        name="solve",
    )(feat, ridge, s, high, low)


def feat_of(y, x, c):
    return ((y % SIDE) * SIDE + x % SIDE) * 2 + c


def permute(value, pairs):
    return lax.ppermute(value, "feat", pairs)


def share_panel(weights, earlier, tail, y, x, c):
    side = range(SIDE)
    root = (feat_of(0, 0, 0), feat_of(0, 0, 1))
    other = permute(earlier[:PANEL, PANEL:3 * PANEL], [root])

    def first_half(k):
        return weights[256 * k:256 * k + 256] if k < 2 else earlier[256 * (k - 2):256 * (k - 1), :PANEL]

    def last_half(k):
        return other[256 * (k % 2):256 * (k % 2) + 256, PANEL * (k // 2):PANEL * (k // 2) + PANEL]

    half = [jnp.where(c == 0, first_half(k), last_half(k)) for k in side]
    got = [permute(half[k], [(root[0], feat_of(0, k, 0)), (root[1], feat_of(k, 0, 1))]) for k in (2, 1, 3)]
    held = jnp.where((x == 0) & (y == 0), half[0], got[0] + got[1] + got[2])
    held = jnp.concatenate([held, tail])
    got = [
        permute(
            held,
            [(feat_of(0, j, 0), feat_of(k, j, 0)) for j in side] + [(feat_of(j, 0, 1), feat_of(j, k, 1)) for j in side],
        )
        for k in (2, 1, 3)
    ]
    held = jnp.where(jnp.where(c == 0, y, x) == 0, held, got[0] + got[1] + got[2])
    got = {
        k: permute(
            held,
            [(feat_of(i, j, 0), feat_of(i, j + k, 0)) for i in side for j in side]
            + [(feat_of(i, j, 1), feat_of(i + k, j, 1)) for i in side for j in side],
        )
        for k in (2, 1, 3)
    }
    own = [held, got[1], got[2], got[3]]
    partner = [permute(own[k], [(i, i ^ 1) for i in range(2 * SIDE * SIDE)]) for k in side]
    return own + partner


def on_device(data, omega, phase, earlier, ridge):
    samp, planes = lax.axis_size("samp"), lax.axis_size("feat")
    scale = math.sqrt(2.0 / (data.shape[0] * samp))
    feat = lax.axis_index("feat")
    y, x, c = place_of(feat)
    feat = feat.reshape(1)

    weights = omega.T
    turns = phase * INV_TURN
    first = lax.reduce_precision(turns, 8, 7)
    second = lax.reduce_precision(turns - first, 8, 7)
    third = turns - first - second
    tail = jnp.stack([first[:PANEL], second[:PANEL], third[:PANEL]]).astype(jnp.bfloat16)
    tail = jnp.concatenate([tail, jnp.zeros((EXTRA - 3, PANEL), jnp.bfloat16)])
    slots = share_panel(weights, earlier, tail, y, x, c)

    local = None
    blocks = data.shape[0] // SAMPLE_BLOCK
    edges = (0, blocks // 4, 5 * blocks // 8, blocks)
    for part in range(3):
        count = edges[part + 1] - edges[part]
        local = local_features(weights, turns[None], data, scale, edges[part], count, SAMPLE_BLOCK, local)
    s, d = gram(feat, slots, *[pltpu.with_memory_space_constraint(v, pltpu.HBM) for v in (data, local, earlier)], scale, samp)
    summed = lax.psum(s, "samp")
    d = lax.all_to_all(d, "samp", 0, 0).sum(0)
    d = lax.all_to_all(jnp.broadcast_to(d, (planes, 16, PANEL)), "feat", 0, 0)
    high, low = factor_inverse(ridge, d)
    return solve(feat, ridge, summed, high, low)


def solution(mesh):
    in_specs = (P("samp", None), P(None, "feat"), P("feat"), P("feat", "samp"), P())
    out_specs = P("feat", None)
    return jax.shard_map(on_device, mesh=mesh, in_specs=in_specs, out_specs=out_specs, check_vma=False)
```

profile of v0, /device:TPU:1, one launch (start us, length us, event | category | flops | bytes accessed | tf_op | source)
XLA Modules:
  0.0 189.5 jit_solution(16084782964157223048)
XLA Ops:
  6.5 1.3 slice.40
  7.8 0.0 copy-start.3
  7.8 1.3 collective-permute-start
  9.2 1.4 copy.8
  10.6 0.0 copy-start.2
  10.6 3.9 %collective-permute-done = bf16[512,1024]{1,0:T(8,128)(2,1)S(1)} collective-permute-done((bf16[512,1024]{1,0:T(8,128)(2,1)S(1)}, bf16[512,1024]{1,0:T(8,128)(2,1)S(1)}, u32[]{:S(2)}, u32[]{:S(2)}) %collective-permute-start) | collective-permute-done | bytes 1048608 | tf_op jit(solution)/shard_map/ppermute | solution.py:341
  14.5 1.1 slice_select_fusion.2
  15.6 1.5 collective-permute-start.1
  17.1 1.3 collective-permute-start.2
  18.4 1.3 collective-permute-start.3
  19.8 0.5 collective-permute-done.1
  20.4 2.8 %collective-permute-done.2 = bf16[256,512]{1,0:T(8,128)(2,1)S(1)} collective-permute-done((bf16[256,512]{1,0:T(8,128)(2,1)S(1)}, bf16[256,512]{1,0:T(8,128)(2,1)S(1)}, u32[]{:S(2)}, u32[]{:S(2)}) %collective-permute-start.2) | collective-permute-done | bytes 262176 | tf_op jit(solution)/shard_map/ppermute | solution.py:341
  23.2 0.0 collective-permute-done.3
  23.2 0.1 fusion
  23.3 0.3 concatenate.4
  23.5 1.3 collective-permute-start.4
  24.8 1.3 collective-permute-start.5
  26.1 1.3 collective-permute-start.6
  27.5 0.8 collective-permute-done.4
  28.3 3.0 %collective-permute-done.5 = bf16[272,512]{1,0:T(8,128)(2,1)S(1)} collective-permute-done((bf16[272,512]{1,0:T(8,128)(2,1)S(1)}, bf16[272,512]{1,0:T(8,128)(2,1)S(1)}, u32[]{:S(2)}, u32[]{:S(2)}) %collective-permute-start.5) | collective-permute-done | bytes 278560 | tf_op jit(solution)/shard_map/ppermute | solution.py:341
  31.3 0.0 collective-permute-done.6
  31.3 0.1 add_select_fusion.refs_0_
  31.3 2.0 %collective-permute-start.7 = (bf16[272,512]{1,0:T(8,128)(2,1)S(1)}, bf16[272,512]{1,0:T(8,128)(2,1)S(1)}, u32[]{:S(2)}, u32[]{:S(2)}) collective-permute-start(bf16[272,512]{1,0:T(8,128)(2,1)S(1)} %add_select_fusion.refs_0_), channel_id=1, source_target_pairs={{0,2},{2,4},{4,6},{6,0},{8,10},{10,12},{12,14},{14,8},{16,18},{18,... | collective-permute-start | bytes 835592 | tf_op jit(solution)/shard_map/ppermute | solution.py:341
  33.3 2.2 %collective-permute-start.8 = (bf16[272,512]{1,0:T(8,128)(2,1)S(1)}, bf16[272,512]{1,0:T(8,128)(2,1)S(1)}, u32[]{:S(2)}, u32[]{:S(2)}) collective-permute-start(bf16[272,512]{1,0:T(8,128)(2,1)S(1)} %add_select_fusion.refs_0_), channel_id=1, source_target_pairs={{0,4},{2,6},{4,0},{6,2},{8,12},{10,14},{12,8},{14,10},{16,20},{18,... | collective-permute-start | bytes 835592 | tf_op jit(solution)/shard_map/ppermute | solution.py:341
  35.5 0.3 collective-permute-start.9
  35.8 0.6 broadcast_in_dim.12.ph_ref
  36.4 2.8 %collective-permute-start.10 = (bf16[272,512]{1,0:T(8,128)(2,1)S(1)}, bf16[272,512]{1,0:T(8,128)(2,1)S(1)}, u32[]{:S(2)}, u32[]{:S(2)}) collective-permute-start(bf16[272,512]{1,0:T(8,128)(2,1)S(1)} %add_select_fusion.refs_0_), channel_id=1, source_target_pairs={{0,1},{1,0},{2,3},{3,2},{4,5},{5,4},{6,7},{7,6},{8,9},{9,8},{10,11... | collective-permute-start | bytes 835592 | tf_op jit(solution)/shard_map/ppermute | solution.py:341
  39.2 0.0 collective-permute-done.7.refs_1_
  39.2 2.2 %collective-permute-start.11 = (bf16[272,512]{1,0:T(8,128)(2,1)S(1)}, bf16[272,512]{1,0:T(8,128)(2,1)S(1)}, u32[]{:S(2)}, u32[]{:S(2)}) collective-permute-start(bf16[272,512]{1,0:T(8,128)(2,1)S(1)} %collective-permute-done.7.refs_1_), channel_id=1, source_target_pairs={{0,1},{1,0},{2,3},{3,2},{4,5},{5,4},{6,7},{7,6},{8,9},{9,8},{10,11... | collective-permute-start | bytes 835592 | tf_op jit(solution)/shard_map/ppermute | solution.py:341
  41.4 1.4 collective-permute-done.8.refs_2_
  42.8 3.1 %collective-permute-start.12 = (bf16[272,512]{1,0:T(8,128)(2,1)S(1)}, bf16[272,512]{1,0:T(8,128)(2,1)S(1)}, u32[]{:S(2)}, u32[]{:S(2)}) collective-permute-start(bf16[272,512]{1,0:T(8,128)(2,1)S(1)} %collective-permute-done.8.refs_2_), channel_id=1, source_target_pairs={{0,1},{1,0},{2,3},{3,2},{4,5},{5,4},{6,7},{7,6},{8,9},{9,8},{10,11... | collective-permute-start | bytes 835592 | tf_op jit(solution)/shard_map/ppermute | solution.py:341
  45.8 0.0 collective-permute-start.13
  45.8 4.5 %local_features.3.refs_0_ = bf16[768,4096]{1,0:T(8,128)(2,1)} custom-call(bf16[768,512]{1,0:T(8,128)(2,1)} %bitcast.4, f32[1,768]{1,0:T(1,128)} %broadcast_in_dim.12.ph_ref, bf16[4096,512]{1,0:T(8,128)(2,1)} %refs_8_.1), custom_call_target="tpu_custom_call" | custom-call | flops 805306368 | bytes 1572864 | tf_op jit(solution)/shard_map/local_features/pallas_call | solution.py:72
  50.4 5.9 %local_features.4.refs_0_ = bf16[768,4096]{1,0:T(8,128)(2,1)} custom-call(bf16[768,512]{1,0:T(8,128)(2,1)} %bitcast.5, f32[1,768]{1,0:T(1,128)} %broadcast_in_dim.12.ph_ref, bf16[4096,512]{1,0:T(8,128)(2,1)} %refs_8_.1, bf16[768,4096]{1,0:T(8,128)(2,1)} %local_features.3.refs_0_), custom_call_target="tpu_custom_call", output_to_operand_aliasing={{}: (3, {})} | custom-call | flops 1207959552 | bytes 2359296 | tf_op jit(solution)/shard_map/local_features/pallas_call | solution.py:72
  56.3 6.0 %local_features.5.refs_9_ = bf16[768,4096]{1,0:T(8,128)(2,1)} custom-call(bf16[768,512]{1,0:T(8,128)(2,1)} %bitcast.6, f32[1,768]{1,0:T(1,128)} %broadcast_in_dim.12.ph_ref, bf16[4096,512]{1,0:T(8,128)(2,1)} %refs_8_.1, bf16[768,4096]{1,0:T(8,128)(2,1)} %local_features.4.refs_0_), custom_call_target="tpu_custom_call", output_to_operand_aliasing={{}: (3, {})} | custom-call | flops 1207959552 | bytes 2359296 | tf_op jit(solution)/shard_map/local_features/pallas_call | solution.py:72
  62.3 0.0 collective-permute-done.12.refs_6_
  62.3 14.4 %gram.1 = (f32[768,512]{1,0:T(8,128)}, f32[8,16,512]{2,1,0:T(8,128)S(1)}) custom-call(s32[1]{0:T(128)} %bitcast.feat_ref, bf16[272,512]{1,0:T(8,128)(2,1)S(1)} %add_select_fusion.refs_0_, bf16[272,512]{1,0:T(8,128)(2,1)S(1)} %collective-permute-done.7.refs_1_, bf16[272,512]{1,0:T(8,128)(2,1)S(1)} %collective-permute-done.8.refs_2_, ...), custom_call_target="tpu_custom_call" | custom-call | flops 8589934592 | bytes 16777216 | tf_op jit(solution)/shard_map/gram/pallas_call | solution.py:150
  76.7 18.7 %all_to_all.10 = f32[8,16,512]{2,1,0:T(8,128)S(1)} all-to-all(f32[8,16,512]{2,1,0:T(8,128)S(1)} %get-tuple-element.10), channel_id=1, replica_groups=mesh['samp'=8,'feat'=32] {'samp'}, dimensions={0} | all-to-all | bytes 524288 | tf_op jit(solution)/shard_map/all_to_all | solution.py:404
  95.4 1.1 broadcast_in_dim.13
  96.5 8.5 %all-to-all-start.1 = ((f32[32,16,512]{2,1,0:T(8,128)}), f32[32,16,512]{2,1,0:T(8,128)S(1)}, u32[]{:S(2)}, u32[]{:S(2)}) async-start(f32[32,16,512]{2,1,0:T(8,128)} %broadcast_in_dim.13), calls=%async_computation.1 | async-start | bytes 2097152 | tf_op jit(solution)/shard_map/all_to_all | solution.py:405
  105.0 0.0 all-reduce.2.cloned.1.call-start
  105.0 0.7 all-reduce.2.cloned.1.call-update
  106.4 15.7 %all-to-all-done.1.d_ref = f32[32,16,512]{2,1,0:T(8,128)S(1)} async-done(((f32[32,16,512]{2,1,0:T(8,128)}), f32[32,16,512]{2,1,0:T(8,128)S(1)}, u32[]{:S(2)}, u32[]{:S(2)}) %all-to-all-start.1) | async-done | bytes 1048608 | tf_op jit(solution)/shard_map/all_to_all | solution.py:405
  122.0 27.2 %factor_inverse.1 = (bf16[512,512]{1,0:T(8,128)(2,1)S(1)}, bf16[512,512]{1,0:T(8,128)(2,1)S(1)}) custom-call(f32[1]{0:T(128)S(6)} %copy.12.ridge_ref, f32[32,16,512]{2,1,0:T(8,128)S(1)} %all-to-all-done.1.d_ref), custom_call_target="tpu_custom_call" | custom-call | flops 8589934592 | bytes 2097152 | tf_op jit(solution)/shard_map/factor_inverse/pallas_call | solution.py:292
  149.3 0.8 copy-done
  150.1 0.8 copy-done.1
  150.9 28.1 %all-reduce.2.cloned.1.call-done.s_ref = f32[768,512]{1,0:T(8,128)} async-done(((f32[768,512]{1,0:T(8,128)}), f32[768,512]{1,0:T(8,128)}) %all-reduce.2.cloned.1.call-update) | async-done | bytes 1572880 | tf_op jit(solution)/shard_map/psum | solution.py:403
  179.0 3.7 %solve.1 = f32[768,512]{1,0:T(8,128)} custom-call(s32[1]{0:T(128)} %bitcast.feat_ref, f32[1]{0:T(128)S(6)} %copy.12.ridge_ref, f32[768,512]{1,0:T(8,128)} %all-reduce.2.cloned.1.call-done.s_ref, bf16[512,512]{1,0:T(8,128)(2,1)} %copy-done, bf16[512,512]{1,0:T(8,128)(2,1)} %copy-done.1), custom_call_target="tpu_custom_call" | custom-call | flops 1207959552 | bytes 4194304 | tf_op jit(solution)/shard_map/solve/pallas_call | solution.py:324
  (17 shorter events, 0.1 us)
Async XLA Ops:
  7.8 11.9 %copy-start.3 = (f32[768]{0:T(1024)S(1)}, f32[768]{0:T(1024)}, u32[]{:S(2)}) copy-start(f32[768]{0:T(1024)} %param.7) | copy-start | bytes 9220
  7.8 6.6 %collective-permute-start = (bf16[512,1024]{1,0:T(8,128)(2,1)S(1)}, bf16[512,1024]{1,0:T(8,128)(2,1)S(1)}, u32[]{:S(2)}, u32[]{:S(2)}) collective-permute-start(bf16[512,1024]{1,0:T(8,128)(2,1)S(1)} %slice.40), channel_id=1, source_target_pairs={{0,1},{32,33},{64,65},{96,97},{128,129},{160,161},{192,193},{224,2... | collective-permute-start | bytes 3145736 | tf_op jit(solution)/shard_map/ppermute | solution.py:341
  10.6 20.8 %copy-start.2 = (bf16[512,768]{0,1:T(8,128)(2,1)}, bf16[512,768]{0,1:T(8,128)(2,1)S(1)}, u32[]{:S(2)}) copy-start(bf16[512,768]{0,1:T(8,128)(2,1)S(1)} %copy.8) | copy-start | bytes 2359300
  15.6 4.8 %collective-permute-start.1 = (bf16[256,512]{1,0:T(8,128)(2,1)S(1)}, bf16[256,512]{1,0:T(8,128)(2,1)S(1)}, u32[]{:S(2)}, u32[]{:S(2)}) collective-permute-start(bf16[256,512]{1,0:T(8,128)(2,1)S(1)} %get-tuple-element.13), channel_id=1, source_target_pairs={{0,4},{1,17},{32,36},{33,49},{64,68},{65,81},{96,100},{97,113},{12... | collective-permute-start | bytes 786440 | tf_op jit(solution)/shard_map/ppermute | solution.py:341
  17.1 6.1 %collective-permute-start.2 = (bf16[256,512]{1,0:T(8,128)(2,1)S(1)}, bf16[256,512]{1,0:T(8,128)(2,1)S(1)}, u32[]{:S(2)}, u32[]{:S(2)}) collective-permute-start(bf16[256,512]{1,0:T(8,128)(2,1)S(1)} %get-tuple-element.15), channel_id=1, source_target_pairs={{0,2},{1,9},{32,34},{33,41},{64,66},{65,73},{96,98},{97,105},{128,... | collective-permute-start | bytes 786440 | tf_op jit(solution)/shard_map/ppermute | solution.py:341
  18.4 4.8 %collective-permute-start.3 = (bf16[256,512]{1,0:T(8,128)(2,1)S(1)}, bf16[256,512]{1,0:T(8,128)(2,1)S(1)}, u32[]{:S(2)}, u32[]{:S(2)}) collective-permute-start(bf16[256,512]{1,0:T(8,128)(2,1)S(1)} %get-tuple-element.14), channel_id=1, source_target_pairs={{0,6},{1,25},{32,38},{33,57},{64,70},{65,89},{96,102},{97,121},{12... | collective-permute-start | bytes 786440 | tf_op jit(solution)/shard_map/ppermute | solution.py:341
  23.5 4.8 %collective-permute-start.4 = (bf16[272,512]{1,0:T(8,128)(2,1)S(1)}, bf16[272,512]{1,0:T(8,128)(2,1)S(1)}, u32[]{:S(2)}, u32[]{:S(2)}) collective-permute-start(bf16[272,512]{1,0:T(8,128)(2,1)S(1)} %concatenate.4), channel_id=1, source_target_pairs={{0,16},{2,18},{4,20},{6,22},{1,5},{9,13},{17,21},{25,29},{32,48},{... | collective-permute-start | bytes 835592 | tf_op jit(solution)/shard_map/ppermute | solution.py:341
  24.8 6.4 %collective-permute-start.5 = (bf16[272,512]{1,0:T(8,128)(2,1)S(1)}, bf16[272,512]{1,0:T(8,128)(2,1)S(1)}, u32[]{:S(2)}, u32[]{:S(2)}) collective-permute-start(bf16[272,512]{1,0:T(8,128)(2,1)S(1)} %concatenate.4), channel_id=1, source_target_pairs={{0,8},{2,10},{4,12},{6,14},{1,3},{9,11},{17,19},{25,27},{32,40},{3... | collective-permute-start | bytes 835592 | tf_op jit(solution)/shard_map/ppermute | solution.py:341
  26.1 5.1 %collective-permute-start.6 = (bf16[272,512]{1,0:T(8,128)(2,1)S(1)}, bf16[272,512]{1,0:T(8,128)(2,1)S(1)}, u32[]{:S(2)}, u32[]{:S(2)}) collective-permute-start(bf16[272,512]{1,0:T(8,128)(2,1)S(1)} %concatenate.4), channel_id=1, source_target_pairs={{0,24},{2,26},{4,28},{6,30},{1,7},{9,15},{17,23},{25,31},{32,56},{... | collective-permute-start | bytes 835592 | tf_op jit(solution)/shard_map/ppermute | solution.py:341
  31.3 7.9 %collective-permute-start.7 = (bf16[272,512]{1,0:T(8,128)(2,1)S(1)}, bf16[272,512]{1,0:T(8,128)(2,1)S(1)}, u32[]{:S(2)}, u32[]{:S(2)}) collective-permute-start(bf16[272,512]{1,0:T(8,128)(2,1)S(1)} %add_select_fusion.refs_0_), channel_id=1, source_target_pairs={{0,2},{2,4},{4,6},{6,0},{8,10},{10,12},{12,14},{14,8},{16,18},{18,... | collective-permute-start | bytes 835592 | tf_op jit(solution)/shard_map/ppermute | solution.py:341
  33.3 9.4 %collective-permute-start.8 = (bf16[272,512]{1,0:T(8,128)(2,1)S(1)}, bf16[272,512]{1,0:T(8,128)(2,1)S(1)}, u32[]{:S(2)}, u32[]{:S(2)}) collective-permute-start(bf16[272,512]{1,0:T(8,128)(2,1)S(1)} %add_select_fusion.refs_0_), channel_id=1, source_target_pairs={{0,4},{2,6},{4,0},{6,2},{8,12},{10,14},{12,8},{14,10},{16,20},{18,... | collective-permute-start | bytes 835592 | tf_op jit(solution)/shard_map/ppermute | solution.py:341
  35.5 10.3 %collective-permute-start.9 = (bf16[272,512]{1,0:T(8,128)(2,1)S(1)}, bf16[272,512]{1,0:T(8,128)(2,1)S(1)}, u32[]{:S(2)}, u32[]{:S(2)}) collective-permute-start(bf16[272,512]{1,0:T(8,128)(2,1)S(1)} %add_select_fusion.refs_0_), channel_id=1, source_target_pairs={{0,6},{2,0},{4,2},{6,4},{8,14},{10,8},{12,10},{14,12},{16,22},{18,... | collective-permute-start | bytes 835592 | tf_op jit(solution)/shard_map/ppermute | solution.py:341
  36.4 25.8 %collective-permute-start.10 = (bf16[272,512]{1,0:T(8,128)(2,1)S(1)}, bf16[272,512]{1,0:T(8,128)(2,1)S(1)}, u32[]{:S(2)}, u32[]{:S(2)}) collective-permute-start(bf16[272,512]{1,0:T(8,128)(2,1)S(1)} %add_select_fusion.refs_0_), channel_id=1, source_target_pairs={{0,1},{1,0},{2,3},{3,2},{4,5},{5,4},{6,7},{7,6},{8,9},{9,8},{10,11... | collective-permute-start | bytes 835592 | tf_op jit(solution)/shard_map/ppermute | solution.py:341
  39.2 23.0 %collective-permute-start.11 = (bf16[272,512]{1,0:T(8,128)(2,1)S(1)}, bf16[272,512]{1,0:T(8,128)(2,1)S(1)}, u32[]{:S(2)}, u32[]{:S(2)}) collective-permute-start(bf16[272,512]{1,0:T(8,128)(2,1)S(1)} %collective-permute-done.7.refs_1_), channel_id=1, source_target_pairs={{0,1},{1,0},{2,3},{3,2},{4,5},{5,4},{6,7},{7,6},{8,9},{9,8},{10,11... | collective-permute-start | bytes 835592 | tf_op jit(solution)/shard_map/ppermute | solution.py:341
  42.8 19.5 %collective-permute-start.12 = (bf16[272,512]{1,0:T(8,128)(2,1)S(1)}, bf16[272,512]{1,0:T(8,128)(2,1)S(1)}, u32[]{:S(2)}, u32[]{:S(2)}) collective-permute-start(bf16[272,512]{1,0:T(8,128)(2,1)S(1)} %collective-permute-done.8.refs_2_), channel_id=1, source_target_pairs={{0,1},{1,0},{2,3},{3,2},{4,5},{5,4},{6,7},{7,6},{8,9},{9,8},{10,11... | collective-permute-start | bytes 835592 | tf_op jit(solution)/shard_map/ppermute | solution.py:341
  45.8 16.4 %collective-permute-start.13 = (bf16[272,512]{1,0:T(8,128)(2,1)S(1)}, bf16[272,512]{1,0:T(8,128)(2,1)S(1)}, u32[]{:S(2)}, u32[]{:S(2)}) collective-permute-start(bf16[272,512]{1,0:T(8,128)(2,1)S(1)} %collective-permute-done.9.refs_3_), channel_id=1, source_target_pairs={{0,1},{1,0},{2,3},{3,2},{4,5},{5,4},{6,7},{7,6},{8,9},{9,8},{10,11... | collective-permute-start | bytes 835592 | tf_op jit(solution)/shard_map/ppermute | solution.py:341
  96.5 25.5 %all-to-all-start.1 = ((f32[32,16,512]{2,1,0:T(8,128)}), f32[32,16,512]{2,1,0:T(8,128)S(1)}, u32[]{:S(2)}, u32[]{:S(2)}) async-start(f32[32,16,512]{2,1,0:T(8,128)} %broadcast_in_dim.13), calls=%async_computation.1 | async-start | bytes 2097152 | tf_op jit(solution)/shard_map/all_to_all | solution.py:405
  105.0 74.0 %all-reduce.2.cloned.1.call-start = ((), (), s32[]{:S(2)}) async-start(), calls=%async_computation.2 | async-start | bytes 3145728 | tf_op jit(solution)/shard_map/psum | solution.py:403
  149.3 0.8 copy-start
  150.1 0.8 copy-start.1
Sparse Core Ops, SparseCore 0:
  108.2 70.7 all-reduce.1
where the time goes:
time: 193 us; the launch traced here: 190 us
  Pallas kernels  61.8 us (32%)
  waiting for transfers between devices  56.8 us (29%)
  starting transfers between devices  30.3 us (16%)
  blocking collectives  18.7 us (10%)
  between operations  14.3 us (7%)
  local copies, waits for them, and re-layouts  6.3 us (3%)
    psum x1, waiting for transfers between devices, on_device(): summed = lax.psum(s, 'samp')  28.1 us
    pallas_call x1, Pallas kernels, factor_inverse(): pl.pallas_call(factor_kernel, out_shape=[jax.ShapeDtypeStruct((n, n), jnp...  27.2 us
    ppermute x14, starting transfers between devices, permute(): return lax.ppermute(value, 'feat', pairs)  21.8 us
    all_to_all x1, blocking collectives, on_device(): d = lax.all_to_all(d, 'samp', 0, 0).sum(0)  18.7 us
    pallas_call x3, Pallas kernels, local_features(): pl.pallas_call(functools.partial(local_kernel, scale=scale), grid=(blocks...  16.4 us
    all_to_all x1, waiting for transfers between devices, on_device(): d = lax.all_to_all(jnp.broadcast_to(d, (planes, 16, PANEL)), 'feat', 0, 0)  15.7 us
    pallas_call x1, Pallas kernels, gram(): pl.pallas_call(functools.partial(gram_kernel, scale=scale, sub=sub), grid...  14.4 us
    ppermute x14, waiting for transfers between devices, permute(): return lax.ppermute(value, 'feat', pairs)  12.4 us
  transfers between devices with their start and end apart: 16, of which 8 were waited for; matrix products, arithmetic and copies ran while one was open for 1% of the time, Pallas kernels for 23%

commit v1 on v0

--- a/solution.py
+++ b/solution.py
@@ -102,10 +102,14 @@
         within = pl.ds(pl.multiple_of(lax.rem(first, 256), 16), 16)
         return v_ref[p + lax.div(first, 256), within, :]
 
-    def add(cols, left, right, sign):
+    def add(cols, left, right, negate=False):
         out = lax.dot_general(left, right, NT, preferred_element_type=jnp.float32)
-        s_ref[:, cols] += sign * out[:rows]
-        acc_ref[:, cols] += sign * out[rows:]
+        if negate:
+            s_ref[:, cols] -= out[:rows]
+            acc_ref[:, cols] -= out[rows:]
+        else:
+            s_ref[:, cols] += out[:rows]
+            acc_ref[:, cols] += out[rows:]
 
     @pl.when(i == 0)
     def _():
@@ -124,7 +128,7 @@
         def _(chunk=chunk):
             left = jnp.concatenate([e_ref[...], sixteen(2 + 2 * chunk)], axis=0)
             for h in range(2):
-                add(slice(256 * h, 256 * h + 256), left, v_ref[2 + 2 * chunk + h, :256, :], -1.0)
+                add(slice(256 * h, 256 * h + 256), left, v_ref[2 + 2 * chunk + h, :256, :], negate=True)
 
     for j in range(x_ref.shape[0] // sub):
         at = slice(j * sub, j * sub + sub)
@@ -132,11 +136,13 @@
             half = slice(256 * h, 256 * h + 256)
             proj = lax.dot_general(v_ref[h, :256, :], x_ref[at, :], NT, preferred_element_type=jnp.float32)
             panel_ref[j, half, :] = scaled_cos(proj * INV_TURN + ph_ref[half, :], scale).astype(jnp.bfloat16)
+    for j in range(x_ref.shape[0] // sub):
+        at = slice(j * sub, j * sub + sub)
         mine = panel_ref[j, pl.ds(first, 16), :]
         left = jnp.concatenate([f_ref[:, at], mine], axis=0)
         for h in range(2):
             half = slice(256 * h, 256 * h + 256)
-            add(half, left, panel_ref[j, half, :], 1.0)
+            add(half, left, panel_ref[j, half, :])
 
     @pl.when(i == pl.num_programs(0) - 1)
     def _():
@@ -353,9 +359,10 @@
         return other[256 * (k % 2):256 * (k % 2) + 256, PANEL * (k // 2):PANEL * (k // 2) + PANEL]
 
     half = [jnp.where(c == 0, first_half(k), last_half(k)) for k in side]
+    front = lax.optimization_barrier(jnp.concatenate([half[0], tail]))
     got = [permute(half[k], [(root[0], feat_of(0, k, 0)), (root[1], feat_of(k, 0, 1))]) for k in (2, 1, 3)]
-    held = jnp.where((x == 0) & (y == 0), half[0], got[0] + got[1] + got[2])
-    held = jnp.concatenate([held, tail])
+    received = jnp.pad(got[0] + got[1] + got[2], ((0, EXTRA), (0, 0)))
+    held = jnp.where((x == 0) & (y == 0), front, received)
     got = [
         permute(
             held,

time: 193 us -> 193 us (level)
  no operation moved by 1% of the time
where the time goes in v1:
time: 193 us; the launch traced here: 189 us
  Pallas kernels  61.3 us (32%)
  waiting for transfers between devices  56.5 us (29%)
  starting transfers between devices  30.3 us (16%)
  blocking collectives  18.7 us (10%)
  between operations  14.3 us (7%)
  local copies, waits for them, and re-layouts  6.31 us (3%)
    psum x1, waiting for transfers between devices, on_device(): summed = lax.psum(s, 'samp')  28 us
    pallas_call x1, Pallas kernels, factor_inverse(): pl.pallas_call(factor_kernel, out_shape=[jax.ShapeDtypeStruct((n, n), jnp...  27.2 us
    ppermute x14, starting transfers between devices, permute(): return lax.ppermute(value, 'feat', pairs)  21.9 us
    all_to_all x1, blocking collectives, on_device(): d = lax.all_to_all(d, 'samp', 0, 0).sum(0)  18.7 us
    pallas_call x3, Pallas kernels, local_features(): pl.pallas_call(functools.partial(local_kernel, scale=scale), grid=(blocks...  16.4 us
    all_to_all x1, waiting for transfers between devices, on_device(): d = lax.all_to_all(jnp.broadcast_to(d, (planes, 16, PANEL)), 'feat', 0, 0)  15.7 us
    pallas_call x1, Pallas kernels, gram(): pl.pallas_call(functools.partial(gram_kernel, scale=scale, sub=sub), grid...  13.9 us
    ppermute x14, waiting for transfers between devices, permute(): return lax.ppermute(value, 'feat', pairs)  12.1 us
  transfers between devices with their start and end apart: 16, of which 8 were waited for; matrix products, arithmetic and copies ran while one was open for 1% of the time, Pallas kernels for 23%

profile of v1, /device:TPU:1, one launch (start us, length us, event | category | flops | bytes accessed | tf_op | source)
XLA Modules:
  0.0 188.8 jit_solution(4035392232417686876)
XLA Ops:
  6.5 1.3 slice.40
  7.8 1.3 collective-permute-start
  9.1 0.0 copy-start.3
  9.2 1.4 copy.8
  10.6 0.0 copy-start.2
  10.6 3.9 %collective-permute-done = bf16[512,1024]{1,0:T(8,128)(2,1)S(1)} collective-permute-done((bf16[512,1024]{1,0:T(8,128)(2,1)S(1)}, bf16[512,1024]{1,0:T(8,128)(2,1)S(1)}, u32[]{:S(2)}, u32[]{:S(2)}) %collective-permute-start) | collective-permute-done | bytes 1048608 | tf_op jit(solution)/shard_map/ppermute | solution.py:347
  14.5 1.1 slice_select_fusion.1
  15.6 1.5 collective-permute-start.1
  17.1 1.3 collective-permute-start.2
  18.4 1.3 collective-permute-start.3
  19.9 0.3 concatenate.4
  20.1 0.3 collective-permute-done.1
  20.4 2.8 %collective-permute-done.2 = bf16[256,512]{1,0:T(8,128)(2,1)S(1)} collective-permute-done((bf16[256,512]{1,0:T(8,128)(2,1)S(1)}, bf16[256,512]{1,0:T(8,128)(2,1)S(1)}, u32[]{:S(2)}, u32[]{:S(2)}) %collective-permute-start.2) | collective-permute-done | bytes 262176 | tf_op jit(solution)/shard_map/ppermute | solution.py:347
  23.2 0.0 collective-permute-done.3
  23.3 0.1 pad_select_fusion
  23.3 1.3 collective-permute-start.4
  24.7 1.3 collective-permute-start.5
  26.0 1.3 collective-permute-start.6
  27.3 0.8 collective-permute-done.4
  28.1 3.0 %collective-permute-done.5 = bf16[272,512]{1,0:T(8,128)(2,1)S(1)} collective-permute-done((bf16[272,512]{1,0:T(8,128)(2,1)S(1)}, bf16[272,512]{1,0:T(8,128)(2,1)S(1)}, u32[]{:S(2)}, u32[]{:S(2)}) %collective-permute-start.5) | collective-permute-done | bytes 278560 | tf_op jit(solution)/shard_map/ppermute | solution.py:347
  31.1 0.0 collective-permute-done.6
  31.1 0.1 add_select_fusion.refs_0_
  31.2 2.0 %collective-permute-start.7 = (bf16[272,512]{1,0:T(8,128)(2,1)S(1)}, bf16[272,512]{1,0:T(8,128)(2,1)S(1)}, u32[]{:S(2)}, u32[]{:S(2)}) collective-permute-start(bf16[272,512]{1,0:T(8,128)(2,1)S(1)} %add_select_fusion.refs_0_), channel_id=1, source_target_pairs={{0,2},{2,4},{4,6},{6,0},{8,10},{10,12},{12,14},{14,8},{16,18},{18,... | collective-permute-start | bytes 835592 | tf_op jit(solution)/shard_map/ppermute | solution.py:347
  33.1 2.2 %collective-permute-start.8 = (bf16[272,512]{1,0:T(8,128)(2,1)S(1)}, bf16[272,512]{1,0:T(8,128)(2,1)S(1)}, u32[]{:S(2)}, u32[]{:S(2)}) collective-permute-start(bf16[272,512]{1,0:T(8,128)(2,1)S(1)} %add_select_fusion.refs_0_), channel_id=1, source_target_pairs={{0,4},{2,6},{4,0},{6,2},{8,12},{10,14},{12,8},{14,10},{16,20},{18,... | collective-permute-start | bytes 835592 | tf_op jit(solution)/shard_map/ppermute | solution.py:347
  35.3 0.3 collective-permute-start.9
  35.6 0.6 broadcast_in_dim.12.ph_ref
  36.2 2.8 %collective-permute-start.10 = (bf16[272,512]{1,0:T(8,128)(2,1)S(1)}, bf16[272,512]{1,0:T(8,128)(2,1)S(1)}, u32[]{:S(2)}, u32[]{:S(2)}) collective-permute-start(bf16[272,512]{1,0:T(8,128)(2,1)S(1)} %add_select_fusion.refs_0_), channel_id=1, source_target_pairs={{0,1},{1,0},{2,3},{3,2},{4,5},{5,4},{6,7},{7,6},{8,9},{9,8},{10,11... | collective-permute-start | bytes 835592 | tf_op jit(solution)/shard_map/ppermute | solution.py:347
  39.0 0.0 collective-permute-done.7.refs_1_
  39.0 2.2 %collective-permute-start.11 = (bf16[272,512]{1,0:T(8,128)(2,1)S(1)}, bf16[272,512]{1,0:T(8,128)(2,1)S(1)}, u32[]{:S(2)}, u32[]{:S(2)}) collective-permute-start(bf16[272,512]{1,0:T(8,128)(2,1)S(1)} %collective-permute-done.7.refs_1_), channel_id=1, source_target_pairs={{0,1},{1,0},{2,3},{3,2},{4,5},{5,4},{6,7},{7,6},{8,9},{9,8},{10,11... | collective-permute-start | bytes 835592 | tf_op jit(solution)/shard_map/ppermute | solution.py:347
  41.2 1.4 collective-permute-done.8.refs_2_
  42.6 3.1 %collective-permute-start.12 = (bf16[272,512]{1,0:T(8,128)(2,1)S(1)}, bf16[272,512]{1,0:T(8,128)(2,1)S(1)}, u32[]{:S(2)}, u32[]{:S(2)}) collective-permute-start(bf16[272,512]{1,0:T(8,128)(2,1)S(1)} %collective-permute-done.8.refs_2_), channel_id=1, source_target_pairs={{0,1},{1,0},{2,3},{3,2},{4,5},{5,4},{6,7},{7,6},{8,9},{9,8},{10,11... | collective-permute-start | bytes 835592 | tf_op jit(solution)/shard_map/ppermute | solution.py:347
  45.6 0.0 collective-permute-done.9.refs_3_
  45.6 0.0 collective-permute-start.13
  45.7 4.6 %local_features.3.refs_0_ = bf16[768,4096]{1,0:T(8,128)(2,1)} custom-call(bf16[768,512]{1,0:T(8,128)(2,1)} %bitcast.3, f32[1,768]{1,0:T(1,128)} %broadcast_in_dim.12.ph_ref, bf16[4096,512]{1,0:T(8,128)(2,1)} %refs_8_.1), custom_call_target="tpu_custom_call" | custom-call | flops 805306368 | bytes 1572864 | tf_op jit(solution)/shard_map/local_features/pallas_call | solution.py:72
  50.2 5.9 %local_features.4.refs_0_ = bf16[768,4096]{1,0:T(8,128)(2,1)} custom-call(bf16[768,512]{1,0:T(8,128)(2,1)} %bitcast.4, f32[1,768]{1,0:T(1,128)} %broadcast_in_dim.12.ph_ref, bf16[4096,512]{1,0:T(8,128)(2,1)} %refs_8_.1, bf16[768,4096]{1,0:T(8,128)(2,1)} %local_features.3.refs_0_), custom_call_target="tpu_custom_call", output_to_operand_aliasing={{}: (3, {})} | custom-call | flops 1207959552 | bytes 2359296 | tf_op jit(solution)/shard_map/local_features/pallas_call | solution.py:72
  56.1 6.0 %local_features.5.refs_9_ = bf16[768,4096]{1,0:T(8,128)(2,1)} custom-call(bf16[768,512]{1,0:T(8,128)(2,1)} %bitcast.5, f32[1,768]{1,0:T(1,128)} %broadcast_in_dim.12.ph_ref, bf16[4096,512]{1,0:T(8,128)(2,1)} %refs_8_.1, bf16[768,4096]{1,0:T(8,128)(2,1)} %local_features.4.refs_0_), custom_call_target="tpu_custom_call", output_to_operand_aliasing={{}: (3, {})} | custom-call | flops 1207959552 | bytes 2359296 | tf_op jit(solution)/shard_map/local_features/pallas_call | solution.py:72
  62.1 13.9 %gram.1 = (f32[768,512]{1,0:T(8,128)}, f32[8,16,512]{2,1,0:T(8,128)S(1)}) custom-call(s32[1]{0:T(128)} %bitcast.feat_ref, bf16[272,512]{1,0:T(8,128)(2,1)S(1)} %add_select_fusion.refs_0_, bf16[272,512]{1,0:T(8,128)(2,1)S(1)} %collective-permute-done.7.refs_1_, bf16[272,512]{1,0:T(8,128)(2,1)S(1)} %collective-permute-done.8.refs_2_, ...), custom_call_target="tpu_custom_call" | custom-call | flops 8589934592 | bytes 16777216 | tf_op jit(solution)/shard_map/gram/pallas_call | solution.py:156
  76.0 18.7 %all_to_all.10 = f32[8,16,512]{2,1,0:T(8,128)S(1)} all-to-all(f32[8,16,512]{2,1,0:T(8,128)S(1)} %get-tuple-element.10), channel_id=1, replica_groups=mesh['samp'=8,'feat'=32] {'samp'}, dimensions={0} | all-to-all | bytes 524288 | tf_op jit(solution)/shard_map/all_to_all | solution.py:411
  94.8 1.1 broadcast_in_dim.13
  95.9 8.4 %all-to-all-start.1 = ((f32[32,16,512]{2,1,0:T(8,128)}), f32[32,16,512]{2,1,0:T(8,128)S(1)}, u32[]{:S(2)}, u32[]{:S(2)}) async-start(f32[32,16,512]{2,1,0:T(8,128)} %broadcast_in_dim.13), calls=%async_computation.1 | async-start | bytes 2097152 | tf_op jit(solution)/shard_map/all_to_all | solution.py:412
  104.3 0.0 all-reduce.3.cloned.1.call-start
  104.4 0.7 all-reduce.3.cloned.1.call-update
  105.7 15.7 %all-to-all-done.1.d_ref = f32[32,16,512]{2,1,0:T(8,128)S(1)} async-done(((f32[32,16,512]{2,1,0:T(8,128)}), f32[32,16,512]{2,1,0:T(8,128)S(1)}, u32[]{:S(2)}, u32[]{:S(2)}) %all-to-all-start.1) | async-done | bytes 1048608 | tf_op jit(solution)/shard_map/all_to_all | solution.py:412
  121.4 27.2 %factor_inverse.1 = (bf16[512,512]{1,0:T(8,128)(2,1)S(1)}, bf16[512,512]{1,0:T(8,128)(2,1)S(1)}) custom-call(f32[1]{0:T(128)S(6)} %copy.12.ridge_ref, f32[32,16,512]{2,1,0:T(8,128)S(1)} %all-to-all-done.1.d_ref), custom_call_target="tpu_custom_call" | custom-call | flops 8589934592 | bytes 2097152 | tf_op jit(solution)/shard_map/factor_inverse/pallas_call | solution.py:298
  148.6 0.8 copy-done
  149.4 0.8 copy-done.1
  150.2 28.0 %all-reduce.3.cloned.1.call-done.s_ref = f32[768,512]{1,0:T(8,128)} async-done(((f32[768,512]{1,0:T(8,128)}), f32[768,512]{1,0:T(8,128)}) %all-reduce.3.cloned.1.call-update) | async-done | bytes 1572880 | tf_op jit(solution)/shard_map/psum | solution.py:410
  178.3 3.7 %solve.1 = f32[768,512]{1,0:T(8,128)} custom-call(s32[1]{0:T(128)} %bitcast.feat_ref, f32[1]{0:T(128)S(6)} %copy.12.ridge_ref, f32[768,512]{1,0:T(8,128)} %all-reduce.3.cloned.1.call-done.s_ref, bf16[512,512]{1,0:T(8,128)(2,1)} %copy-done, bf16[512,512]{1,0:T(8,128)(2,1)} %copy-done.1), custom_call_target="tpu_custom_call" | custom-call | flops 1207959552 | bytes 4194304 | tf_op jit(solution)/shard_map/solve/pallas_call | solution.py:330
  (18 shorter events, 0.1 us)
Async XLA Ops:
  7.8 6.6 %collective-permute-start = (bf16[512,1024]{1,0:T(8,128)(2,1)S(1)}, bf16[512,1024]{1,0:T(8,128)(2,1)S(1)}, u32[]{:S(2)}, u32[]{:S(2)}) collective-permute-start(bf16[512,1024]{1,0:T(8,128)(2,1)S(1)} %slice.40), channel_id=1, source_target_pairs={{0,1},{32,33},{64,65},{96,97},{128,129},{160,161},{192,193},{224,2... | collective-permute-start | bytes 3145736 | tf_op jit(solution)/shard_map/ppermute | solution.py:347
  9.1 10.6 %copy-start.3 = (f32[768]{0:T(1024)S(1)}, f32[768]{0:T(1024)}, u32[]{:S(2)}) copy-start(f32[768]{0:T(1024)} %param.7) | copy-start | bytes 9220
  10.6 12.7 %copy-start.2 = (bf16[512,768]{0,1:T(8,128)(2,1)}, bf16[512,768]{0,1:T(8,128)(2,1)S(1)}, u32[]{:S(2)}) copy-start(bf16[512,768]{0,1:T(8,128)(2,1)S(1)} %copy.8) | copy-start | bytes 2359300
  15.6 4.8 %collective-permute-start.1 = (bf16[256,512]{1,0:T(8,128)(2,1)S(1)}, bf16[256,512]{1,0:T(8,128)(2,1)S(1)}, u32[]{:S(2)}, u32[]{:S(2)}) collective-permute-start(bf16[256,512]{1,0:T(8,128)(2,1)S(1)} %get-tuple-element.18), channel_id=1, source_target_pairs={{0,4},{1,17},{32,36},{33,49},{64,68},{65,81},{96,100},{97,113},{12... | collective-permute-start | bytes 786440 | tf_op jit(solution)/shard_map/ppermute | solution.py:347
  17.1 6.1 %collective-permute-start.2 = (bf16[256,512]{1,0:T(8,128)(2,1)S(1)}, bf16[256,512]{1,0:T(8,128)(2,1)S(1)}, u32[]{:S(2)}, u32[]{:S(2)}) collective-permute-start(bf16[256,512]{1,0:T(8,128)(2,1)S(1)} %get-tuple-element.15), channel_id=1, source_target_pairs={{0,2},{1,9},{32,34},{33,41},{64,66},{65,73},{96,98},{97,105},{128,... | collective-permute-start | bytes 786440 | tf_op jit(solution)/shard_map/ppermute | solution.py:347
  18.4 4.8 %collective-permute-start.3 = (bf16[256,512]{1,0:T(8,128)(2,1)S(1)}, bf16[256,512]{1,0:T(8,128)(2,1)S(1)}, u32[]{:S(2)}, u32[]{:S(2)}) collective-permute-start(bf16[256,512]{1,0:T(8,128)(2,1)S(1)} %get-tuple-element.17), channel_id=1, source_target_pairs={{0,6},{1,25},{32,38},{33,57},{64,70},{65,89},{96,102},{97,121},{12... | collective-permute-start | bytes 786440 | tf_op jit(solution)/shard_map/ppermute | solution.py:347
  23.3 4.8 %collective-permute-start.4 = (bf16[272,512]{1,0:T(8,128)(2,1)S(1)}, bf16[272,512]{1,0:T(8,128)(2,1)S(1)}, u32[]{:S(2)}, u32[]{:S(2)}) collective-permute-start(bf16[272,512]{1,0:T(8,128)(2,1)S(1)} %pad_select_fusion), channel_id=1, source_target_pairs={{0,16},{2,18},{4,20},{6,22},{1,5},{9,13},{17,21},{25,29},{32,48},{... | collective-permute-start | bytes 835592 | tf_op jit(solution)/shard_map/ppermute | solution.py:347
  24.7 6.4 %collective-permute-start.5 = (bf16[272,512]{1,0:T(8,128)(2,1)S(1)}, bf16[272,512]{1,0:T(8,128)(2,1)S(1)}, u32[]{:S(2)}, u32[]{:S(2)}) collective-permute-start(bf16[272,512]{1,0:T(8,128)(2,1)S(1)} %pad_select_fusion), channel_id=1, source_target_pairs={{0,8},{2,10},{4,12},{6,14},{1,3},{9,11},{17,19},{25,27},{32,40},{3... | collective-permute-start | bytes 835592 | tf_op jit(solution)/shard_map/ppermute | solution.py:347
  26.0 5.1 %collective-permute-start.6 = (bf16[272,512]{1,0:T(8,128)(2,1)S(1)}, bf16[272,512]{1,0:T(8,128)(2,1)S(1)}, u32[]{:S(2)}, u32[]{:S(2)}) collective-permute-start(bf16[272,512]{1,0:T(8,128)(2,1)S(1)} %pad_select_fusion), channel_id=1, source_target_pairs={{0,24},{2,26},{4,28},{6,30},{1,7},{9,15},{17,23},{25,31},{32,56},{... | collective-permute-start | bytes 835592 | tf_op jit(solution)/shard_map/ppermute | solution.py:347
  31.2 7.9 %collective-permute-start.7 = (bf16[272,512]{1,0:T(8,128)(2,1)S(1)}, bf16[272,512]{1,0:T(8,128)(2,1)S(1)}, u32[]{:S(2)}, u32[]{:S(2)}) collective-permute-start(bf16[272,512]{1,0:T(8,128)(2,1)S(1)} %add_select_fusion.refs_0_), channel_id=1, source_target_pairs={{0,2},{2,4},{4,6},{6,0},{8,10},{10,12},{12,14},{14,8},{16,18},{18,... | collective-permute-start | bytes 835592 | tf_op jit(solution)/shard_map/ppermute | solution.py:347
  33.1 9.4 %collective-permute-start.8 = (bf16[272,512]{1,0:T(8,128)(2,1)S(1)}, bf16[272,512]{1,0:T(8,128)(2,1)S(1)}, u32[]{:S(2)}, u32[]{:S(2)}) collective-permute-start(bf16[272,512]{1,0:T(8,128)(2,1)S(1)} %add_select_fusion.refs_0_), channel_id=1, source_target_pairs={{0,4},{2,6},{4,0},{6,2},{8,12},{10,14},{12,8},{14,10},{16,20},{18,... | collective-permute-start | bytes 835592 | tf_op jit(solution)/shard_map/ppermute | solution.py:347
  35.3 10.3 %collective-permute-start.9 = (bf16[272,512]{1,0:T(8,128)(2,1)S(1)}, bf16[272,512]{1,0:T(8,128)(2,1)S(1)}, u32[]{:S(2)}, u32[]{:S(2)}) collective-permute-start(bf16[272,512]{1,0:T(8,128)(2,1)S(1)} %add_select_fusion.refs_0_), channel_id=1, source_target_pairs={{0,6},{2,0},{4,2},{6,4},{8,14},{10,8},{12,10},{14,12},{16,22},{18,... | collective-permute-start | bytes 835592 | tf_op jit(solution)/shard_map/ppermute | solution.py:347
  36.2 25.8 %collective-permute-start.10 = (bf16[272,512]{1,0:T(8,128)(2,1)S(1)}, bf16[272,512]{1,0:T(8,128)(2,1)S(1)}, u32[]{:S(2)}, u32[]{:S(2)}) collective-permute-start(bf16[272,512]{1,0:T(8,128)(2,1)S(1)} %add_select_fusion.refs_0_), channel_id=1, source_target_pairs={{0,1},{1,0},{2,3},{3,2},{4,5},{5,4},{6,7},{7,6},{8,9},{9,8},{10,11... | collective-permute-start | bytes 835592 | tf_op jit(solution)/shard_map/ppermute | solution.py:347
  39.0 23.1 %collective-permute-start.11 = (bf16[272,512]{1,0:T(8,128)(2,1)S(1)}, bf16[272,512]{1,0:T(8,128)(2,1)S(1)}, u32[]{:S(2)}, u32[]{:S(2)}) collective-permute-start(bf16[272,512]{1,0:T(8,128)(2,1)S(1)} %collective-permute-done.7.refs_1_), channel_id=1, source_target_pairs={{0,1},{1,0},{2,3},{3,2},{4,5},{5,4},{6,7},{7,6},{8,9},{9,8},{10,11... | collective-permute-start | bytes 835592 | tf_op jit(solution)/shard_map/ppermute | solution.py:347
  42.6 19.5 %collective-permute-start.12 = (bf16[272,512]{1,0:T(8,128)(2,1)S(1)}, bf16[272,512]{1,0:T(8,128)(2,1)S(1)}, u32[]{:S(2)}, u32[]{:S(2)}) collective-permute-start(bf16[272,512]{1,0:T(8,128)(2,1)S(1)} %collective-permute-done.8.refs_2_), channel_id=1, source_target_pairs={{0,1},{1,0},{2,3},{3,2},{4,5},{5,4},{6,7},{7,6},{8,9},{9,8},{10,11... | collective-permute-start | bytes 835592 | tf_op jit(solution)/shard_map/ppermute | solution.py:347
  45.6 16.5 %collective-permute-start.13 = (bf16[272,512]{1,0:T(8,128)(2,1)S(1)}, bf16[272,512]{1,0:T(8,128)(2,1)S(1)}, u32[]{:S(2)}, u32[]{:S(2)}) collective-permute-start(bf16[272,512]{1,0:T(8,128)(2,1)S(1)} %collective-permute-done.9.refs_3_), channel_id=1, source_target_pairs={{0,1},{1,0},{2,3},{3,2},{4,5},{5,4},{6,7},{7,6},{8,9},{9,8},{10,11... | collective-permute-start | bytes 835592 | tf_op jit(solution)/shard_map/ppermute | solution.py:347
  95.9 25.5 %all-to-all-start.1 = ((f32[32,16,512]{2,1,0:T(8,128)}), f32[32,16,512]{2,1,0:T(8,128)S(1)}, u32[]{:S(2)}, u32[]{:S(2)}) async-start(f32[32,16,512]{2,1,0:T(8,128)} %broadcast_in_dim.13), calls=%async_computation.1 | async-start | bytes 2097152 | tf_op jit(solution)/shard_map/all_to_all | solution.py:412
  104.3 73.9 %all-reduce.3.cloned.1.call-start = ((), (), s32[]{:S(2)}) async-start(), calls=%async_computation.2 | async-start | bytes 3145728 | tf_op jit(solution)/shard_map/psum | solution.py:410
  148.6 0.8 copy-start
  149.4 0.8 copy-start.1
Sparse Core Ops, SparseCore 0:
  107.5 70.7 all-reduce.2

commit v2 on v1

--- a/solution.py
+++ b/solution.py
@@ -360,7 +360,7 @@
 
     half = [jnp.where(c == 0, first_half(k), last_half(k)) for k in side]
     front = lax.optimization_barrier(jnp.concatenate([half[0], tail]))
-    got = [permute(half[k], [(root[0], feat_of(0, k, 0)), (root[1], feat_of(k, 0, 1))]) for k in (2, 1, 3)]
+    got = [permute(half[k], [(root[0], feat_of(0, k, 0)), (root[1], feat_of(k, 0, 1))]) for k in (1, 3, 2)]
     received = jnp.pad(got[0] + got[1] + got[2], ((0, EXTRA), (0, 0)))
     held = jnp.where((x == 0) & (y == 0), front, received)
     got = [
@@ -368,7 +368,7 @@
             held,
             [(feat_of(0, j, 0), feat_of(k, j, 0)) for j in side] + [(feat_of(j, 0, 1), feat_of(j, k, 1)) for j in side],
         )
-        for k in (2, 1, 3)
+        for k in (1, 3, 2)
     ]
     held = jnp.where(jnp.where(c == 0, y, x) == 0, held, got[0] + got[1] + got[2])
     got = {
@@ -377,7 +377,7 @@
             [(feat_of(i, j, 0), feat_of(i, j + k, 0)) for i in side for j in side]
             + [(feat_of(i, j, 1), feat_of(i + k, j, 1)) for i in side for j in side],
         )
-        for k in (2, 1, 3)
+        for k in (1, 3, 2)
     }
     own = [held, got[1], got[2], got[3]]
     partner = [permute(own[k], [(i, i ^ 1) for i in range(2 * SIDE * SIDE)]) for k in side]

time: 193 us -> 194 us (level)
    all_to_all x1, starting transfers between devices: 8.42 us -> 10.8 us  [on_device(): d = lax.all_to_all(jnp.broadcast_to(d, (planes, 16, PANEL)), 'feat', 0, 0)]
  transfers between devices with their start and end apart: 16 -> 16, of which waited for: 8 -> 10; matrix products, arithmetic and copies ran while one was open for 1% -> 1% of each run, Pallas kernels for 23% -> 23%
where the time goes in v2:
time: 194 us; the launch traced here: 190 us
  Pallas kernels  61.3 us (32%)
  waiting for transfers between devices  56.5 us (29%)
  starting transfers between devices  31.4 us (16%)
  blocking collectives  19.3 us (10%)
  between operations  14.3 us (7%)
  local copies, waits for them, and re-layouts  6.31 us (3%)
    psum x1, waiting for transfers between devices, on_device(): summed = lax.psum(s, 'samp')  28 us
    pallas_call x1, Pallas kernels, factor_inverse(): pl.pallas_call(factor_kernel, out_shape=[jax.ShapeDtypeStruct((n, n), jnp...  27.2 us
    ppermute x14, starting transfers between devices, permute(): return lax.ppermute(value, 'feat', pairs)  20.6 us
    all_to_all x1, blocking collectives, on_device(): d = lax.all_to_all(d, 'samp', 0, 0).sum(0)  19.3 us
    pallas_call x3, Pallas kernels, local_features(): pl.pallas_call(functools.partial(local_kernel, scale=scale), grid=(blocks...  16.4 us
    all_to_all x1, waiting for transfers between devices, on_device(): d = lax.all_to_all(jnp.broadcast_to(d, (planes, 16, PANEL)), 'feat', 0, 0)  15.7 us
    pallas_call x1, Pallas kernels, gram(): pl.pallas_call(functools.partial(gram_kernel, scale=scale, sub=sub), grid...  13.9 us
    ppermute x14, waiting for transfers between devices, permute(): return lax.ppermute(value, 'feat', pairs)  12.1 us
  transfers between devices with their start and end apart: 16, of which 10 were waited for; matrix products, arithmetic and copies ran while one was open for 1% of the time, Pallas kernels for 23%

profile of v2, /device:TPU:1, one launch (start us, length us, event | category | flops | bytes accessed | tf_op | source)
XLA Modules:
  0.0 190.5 jit_solution(17365257003801160383)
XLA Ops:
  6.5 1.3 slice.40
  7.8 1.3 collective-permute-start
  9.1 0.0 copy-start.3
  9.2 1.4 copy.8
  10.6 0.0 copy-start.2
  10.6 3.9 %collective-permute-done = bf16[512,1024]{1,0:T(8,128)(2,1)S(1)} collective-permute-done((bf16[512,1024]{1,0:T(8,128)(2,1)S(1)}, bf16[512,1024]{1,0:T(8,128)(2,1)S(1)}, u32[]{:S(2)}, u32[]{:S(2)}) %collective-permute-start) | collective-permute-done | bytes 1048608 | tf_op jit(solution)/shard_map/ppermute | solution.py:347
  14.5 1.1 slice_select_fusion.1
  15.6 1.3 collective-permute-start.1
  16.9 1.3 collective-permute-start.2
  18.2 1.3 collective-permute-start.3
  19.7 0.3 concatenate.4
  19.9 0.3 collective-permute-done.1
  20.2 1.3 collective-permute-done.2
  21.5 1.5 collective-permute-done.3
  23.1 0.1 pad_select_fusion
  23.1 1.3 collective-permute-start.4
  24.5 1.3 collective-permute-start.5
  25.8 1.3 collective-permute-start.6
  27.1 0.8 collective-permute-done.4
  27.9 1.3 collective-permute-done.5
  29.2 1.7 collective-permute-done.6
  30.9 0.1 add_select_fusion.refs_0_
  31.0 0.1 collective-permute-start.7
  31.0 3.5 %collective-permute-start.8 = (bf16[272,512]{1,0:T(8,128)(2,1)S(1)}, bf16[272,512]{1,0:T(8,128)(2,1)S(1)}, u32[]{:S(2)}, u32[]{:S(2)}) collective-permute-start(bf16[272,512]{1,0:T(8,128)(2,1)S(1)} %add_select_fusion.refs_0_), channel_id=1, source_target_pairs={{0,4},{2,6},{4,0},{6,2},{8,12},{10,14},{12,8},{14,10},{16,20},{18,... | collective-permute-start | bytes 835592 | tf_op jit(solution)/shard_map/ppermute | solution.py:347
  34.5 2.0 %collective-permute-start.9 = (bf16[272,512]{1,0:T(8,128)(2,1)S(1)}, bf16[272,512]{1,0:T(8,128)(2,1)S(1)}, u32[]{:S(2)}, u32[]{:S(2)}) collective-permute-start(bf16[272,512]{1,0:T(8,128)(2,1)S(1)} %add_select_fusion.refs_0_), channel_id=1, source_target_pairs={{0,6},{2,0},{4,2},{6,4},{8,14},{10,8},{12,10},{14,12},{16,22},{18,... | collective-permute-start | bytes 835592 | tf_op jit(solution)/shard_map/ppermute | solution.py:347
  36.5 0.6 broadcast_in_dim.12.ph_ref
  37.1 3.0 %collective-permute-start.10 = (bf16[272,512]{1,0:T(8,128)(2,1)S(1)}, bf16[272,512]{1,0:T(8,128)(2,1)S(1)}, u32[]{:S(2)}, u32[]{:S(2)}) collective-permute-start(bf16[272,512]{1,0:T(8,128)(2,1)S(1)} %add_select_fusion.refs_0_), channel_id=1, source_target_pairs={{0,1},{1,0},{2,3},{3,2},{4,5},{5,4},{6,7},{7,6},{8,9},{9,8},{10,11... | collective-permute-start | bytes 835592 | tf_op jit(solution)/shard_map/ppermute | solution.py:347
  40.1 0.2 collective-permute-start.11
  40.3 1.3 collective-permute-done.8.refs_2_
  41.7 2.7 %collective-permute-start.12 = (bf16[272,512]{1,0:T(8,128)(2,1)S(1)}, bf16[272,512]{1,0:T(8,128)(2,1)S(1)}, u32[]{:S(2)}, u32[]{:S(2)}) collective-permute-start(bf16[272,512]{1,0:T(8,128)(2,1)S(1)} %collective-permute-done.8.refs_2_), channel_id=1, source_target_pairs={{0,1},{1,0},{2,3},{3,2},{4,5},{5,4},{6,7},{7,6},{8,9},{9,8},{10,11... | collective-permute-start | bytes 835592 | tf_op jit(solution)/shard_map/ppermute | solution.py:347
  44.3 0.0 collective-permute-done.9.refs_3_
  44.4 0.0 collective-permute-start.13
  44.4 4.5 %local_features.3.refs_0_ = bf16[768,4096]{1,0:T(8,128)(2,1)} custom-call(bf16[768,512]{1,0:T(8,128)(2,1)} %bitcast.3, f32[1,768]{1,0:T(1,128)} %broadcast_in_dim.12.ph_ref, bf16[4096,512]{1,0:T(8,128)(2,1)} %refs_8_.1), custom_call_target="tpu_custom_call" | custom-call | flops 805306368 | bytes 1572864 | tf_op jit(solution)/shard_map/local_features/pallas_call | solution.py:72
  48.9 5.9 %local_features.4.refs_0_ = bf16[768,4096]{1,0:T(8,128)(2,1)} custom-call(bf16[768,512]{1,0:T(8,128)(2,1)} %bitcast.4, f32[1,768]{1,0:T(1,128)} %broadcast_in_dim.12.ph_ref, bf16[4096,512]{1,0:T(8,128)(2,1)} %refs_8_.1, bf16[768,4096]{1,0:T(8,128)(2,1)} %local_features.3.refs_0_), custom_call_target="tpu_custom_call", output_to_operand_aliasing={{}: (3, {})} | custom-call | flops 1207959552 | bytes 2359296 | tf_op jit(solution)/shard_map/local_features/pallas_call | solution.py:72
  54.8 6.0 %local_features.5.refs_9_ = bf16[768,4096]{1,0:T(8,128)(2,1)} custom-call(bf16[768,512]{1,0:T(8,128)(2,1)} %bitcast.5, f32[1,768]{1,0:T(1,128)} %broadcast_in_dim.12.ph_ref, bf16[4096,512]{1,0:T(8,128)(2,1)} %refs_8_.1, bf16[768,4096]{1,0:T(8,128)(2,1)} %local_features.4.refs_0_), custom_call_target="tpu_custom_call", output_to_operand_aliasing={{}: (3, {})} | custom-call | flops 1207959552 | bytes 2359296 | tf_op jit(solution)/shard_map/local_features/pallas_call | solution.py:72
  60.8 0.0 collective-permute-done.11.refs_5_
  60.8 13.9 %gram.1 = (f32[768,512]{1,0:T(8,128)}, f32[8,16,512]{2,1,0:T(8,128)S(1)}) custom-call(s32[1]{0:T(128)} %bitcast.feat_ref, bf16[272,512]{1,0:T(8,128)(2,1)S(1)} %add_select_fusion.refs_0_, bf16[272,512]{1,0:T(8,128)(2,1)S(1)} %collective-permute-done.7.refs_1_, bf16[272,512]{1,0:T(8,128)(2,1)S(1)} %collective-permute-done.8.refs_2_, ...), custom_call_target="tpu_custom_call" | custom-call | flops 8589934592 | bytes 16777216 | tf_op jit(solution)/shard_map/gram/pallas_call | solution.py:156
  74.7 19.3 %all_to_all.10 = f32[8,16,512]{2,1,0:T(8,128)S(1)} all-to-all(f32[8,16,512]{2,1,0:T(8,128)S(1)} %get-tuple-element.10), channel_id=1, replica_groups=mesh['samp'=8,'feat'=32] {'samp'}, dimensions={0} | all-to-all | bytes 524288 | tf_op jit(solution)/shard_map/all_to_all | solution.py:411
  94.1 1.1 broadcast_in_dim.13
  95.2 10.8 %all-to-all-start.1 = ((f32[32,16,512]{2,1,0:T(8,128)}), f32[32,16,512]{2,1,0:T(8,128)S(1)}, u32[]{:S(2)}, u32[]{:S(2)}) async-start(f32[32,16,512]{2,1,0:T(8,128)} %broadcast_in_dim.13), calls=%async_computation.1 | async-start | bytes 2097152 | tf_op jit(solution)/shard_map/all_to_all | solution.py:412
  106.0 0.0 all-reduce.3.cloned.1.call-start
  106.0 0.7 all-reduce.3.cloned.1.call-update
  107.4 15.7 %all-to-all-done.1.d_ref = f32[32,16,512]{2,1,0:T(8,128)S(1)} async-done(((f32[32,16,512]{2,1,0:T(8,128)}), f32[32,16,512]{2,1,0:T(8,128)S(1)}, u32[]{:S(2)}, u32[]{:S(2)}) %all-to-all-start.1) | async-done | bytes 1048608 | tf_op jit(solution)/shard_map/all_to_all | solution.py:412
  123.0 27.2 %factor_inverse.1 = (bf16[512,512]{1,0:T(8,128)(2,1)S(1)}, bf16[512,512]{1,0:T(8,128)(2,1)S(1)}) custom-call(f32[1]{0:T(128)S(6)} %copy.12.ridge_ref, f32[32,16,512]{2,1,0:T(8,128)S(1)} %all-to-all-done.1.d_ref), custom_call_target="tpu_custom_call" | custom-call | flops 8589934592 | bytes 2097152 | tf_op jit(solution)/shard_map/factor_inverse/pallas_call | solution.py:298
  150.3 0.8 copy-done
  151.1 0.8 copy-done.1
  151.9 28.0 %all-reduce.3.cloned.1.call-done.s_ref = f32[768,512]{1,0:T(8,128)} async-done(((f32[768,512]{1,0:T(8,128)}), f32[768,512]{1,0:T(8,128)}) %all-reduce.3.cloned.1.call-update) | async-done | bytes 1572880 | tf_op jit(solution)/shard_map/psum | solution.py:410
  179.9 3.7 %solve.1 = f32[768,512]{1,0:T(8,128)} custom-call(s32[1]{0:T(128)} %bitcast.feat_ref, f32[1]{0:T(128)S(6)} %copy.12.ridge_ref, f32[768,512]{1,0:T(8,128)} %all-reduce.3.cloned.1.call-done.s_ref, bf16[512,512]{1,0:T(8,128)(2,1)} %copy-done, bf16[512,512]{1,0:T(8,128)(2,1)} %copy-done.1), custom_call_target="tpu_custom_call" | custom-call | flops 1207959552 | bytes 4194304 | tf_op jit(solution)/shard_map/solve/pallas_call | solution.py:330
  (18 shorter events, 0.1 us)
Async XLA Ops:
  7.8 6.6 %collective-permute-start = (bf16[512,1024]{1,0:T(8,128)(2,1)S(1)}, bf16[512,1024]{1,0:T(8,128)(2,1)S(1)}, u32[]{:S(2)}, u32[]{:S(2)}) collective-permute-start(bf16[512,1024]{1,0:T(8,128)(2,1)S(1)} %slice.40), channel_id=1, source_target_pairs={{0,1},{32,33},{64,65},{96,97},{128,129},{160,161},{192,193},{224,2... | collective-permute-start | bytes 3145736 | tf_op jit(solution)/shard_map/ppermute | solution.py:347
  9.1 10.4 %copy-start.3 = (f32[768]{0:T(1024)S(1)}, f32[768]{0:T(1024)}, u32[]{:S(2)}) copy-start(f32[768]{0:T(1024)} %param.7) | copy-start | bytes 9220
  10.6 12.5 %copy-start.2 = (bf16[512,768]{0,1:T(8,128)(2,1)}, bf16[512,768]{0,1:T(8,128)(2,1)S(1)}, u32[]{:S(2)}) copy-start(bf16[512,768]{0,1:T(8,128)(2,1)S(1)} %copy.8) | copy-start | bytes 2359300
  15.6 4.6 %collective-permute-start.1 = (bf16[256,512]{1,0:T(8,128)(2,1)S(1)}, bf16[256,512]{1,0:T(8,128)(2,1)S(1)}, u32[]{:S(2)}, u32[]{:S(2)}) collective-permute-start(bf16[256,512]{1,0:T(8,128)(2,1)S(1)} %get-tuple-element.18), channel_id=1, source_target_pairs={{0,2},{1,9},{32,34},{33,41},{64,66},{65,73},{96,98},{97,105},{128,... | collective-permute-start | bytes 786440 | tf_op jit(solution)/shard_map/ppermute | solution.py:347
  16.9 4.6 %collective-permute-start.2 = (bf16[256,512]{1,0:T(8,128)(2,1)S(1)}, bf16[256,512]{1,0:T(8,128)(2,1)S(1)}, u32[]{:S(2)}, u32[]{:S(2)}) collective-permute-start(bf16[256,512]{1,0:T(8,128)(2,1)S(1)} %get-tuple-element.13), channel_id=1, source_target_pairs={{0,6},{1,25},{32,38},{33,57},{64,70},{65,89},{96,102},{97,121},{12... | collective-permute-start | bytes 786440 | tf_op jit(solution)/shard_map/ppermute | solution.py:347
  18.2 4.8 %collective-permute-start.3 = (bf16[256,512]{1,0:T(8,128)(2,1)S(1)}, bf16[256,512]{1,0:T(8,128)(2,1)S(1)}, u32[]{:S(2)}, u32[]{:S(2)}) collective-permute-start(bf16[256,512]{1,0:T(8,128)(2,1)S(1)} %get-tuple-element.14), channel_id=1, source_target_pairs={{0,4},{1,17},{32,36},{33,49},{64,68},{65,81},{96,100},{97,113},{12... | collective-permute-start | bytes 786440 | tf_op jit(solution)/shard_map/ppermute | solution.py:347
  23.1 4.8 %collective-permute-start.4 = (bf16[272,512]{1,0:T(8,128)(2,1)S(1)}, bf16[272,512]{1,0:T(8,128)(2,1)S(1)}, u32[]{:S(2)}, u32[]{:S(2)}) collective-permute-start(bf16[272,512]{1,0:T(8,128)(2,1)S(1)} %pad_select_fusion), channel_id=1, source_target_pairs={{0,8},{2,10},{4,12},{6,14},{1,3},{9,11},{17,19},{25,27},{32,40},{3... | collective-permute-start | bytes 835592 | tf_op jit(solution)/shard_map/ppermute | solution.py:347
  24.5 4.8 %collective-permute-start.5 = (bf16[272,512]{1,0:T(8,128)(2,1)S(1)}, bf16[272,512]{1,0:T(8,128)(2,1)S(1)}, u32[]{:S(2)}, u32[]{:S(2)}) collective-permute-start(bf16[272,512]{1,0:T(8,128)(2,1)S(1)} %pad_select_fusion), channel_id=1, source_target_pairs={{0,24},{2,26},{4,28},{6,30},{1,7},{9,15},{17,23},{25,31},{32,56},{... | collective-permute-start | bytes 835592 | tf_op jit(solution)/shard_map/ppermute | solution.py:347
  25.8 5.1 %collective-permute-start.6 = (bf16[272,512]{1,0:T(8,128)(2,1)S(1)}, bf16[272,512]{1,0:T(8,128)(2,1)S(1)}, u32[]{:S(2)}, u32[]{:S(2)}) collective-permute-start(bf16[272,512]{1,0:T(8,128)(2,1)S(1)} %pad_select_fusion), channel_id=1, source_target_pairs={{0,16},{2,18},{4,20},{6,22},{1,5},{9,13},{17,21},{25,29},{32,48},{... | collective-permute-start | bytes 835592 | tf_op jit(solution)/shard_map/ppermute | solution.py:347
  31.0 9.1 %collective-permute-start.7 = (bf16[272,512]{1,0:T(8,128)(2,1)S(1)}, bf16[272,512]{1,0:T(8,128)(2,1)S(1)}, u32[]{:S(2)}, u32[]{:S(2)}) collective-permute-start(bf16[272,512]{1,0:T(8,128)(2,1)S(1)} %add_select_fusion.refs_0_), channel_id=1, source_target_pairs={{0,2},{2,4},{4,6},{6,0},{8,10},{10,12},{12,14},{14,8},{16,18},{18,... | collective-permute-start | bytes 835592 | tf_op jit(solution)/shard_map/ppermute | solution.py:347
  31.0 10.6 %collective-permute-start.8 = (bf16[272,512]{1,0:T(8,128)(2,1)S(1)}, bf16[272,512]{1,0:T(8,128)(2,1)S(1)}, u32[]{:S(2)}, u32[]{:S(2)}) collective-permute-start(bf16[272,512]{1,0:T(8,128)(2,1)S(1)} %add_select_fusion.refs_0_), channel_id=1, source_target_pairs={{0,4},{2,6},{4,0},{6,2},{8,12},{10,14},{12,8},{14,10},{16,20},{18,... | collective-permute-start | bytes 835592 | tf_op jit(solution)/shard_map/ppermute | solution.py:347
  34.5 9.8 %collective-permute-start.9 = (bf16[272,512]{1,0:T(8,128)(2,1)S(1)}, bf16[272,512]{1,0:T(8,128)(2,1)S(1)}, u32[]{:S(2)}, u32[]{:S(2)}) collective-permute-start(bf16[272,512]{1,0:T(8,128)(2,1)S(1)} %add_select_fusion.refs_0_), channel_id=1, source_target_pairs={{0,6},{2,0},{4,2},{6,4},{8,14},{10,8},{12,10},{14,12},{16,22},{18,... | collective-permute-start | bytes 835592 | tf_op jit(solution)/shard_map/ppermute | solution.py:347
  37.1 23.7 %collective-permute-start.10 = (bf16[272,512]{1,0:T(8,128)(2,1)S(1)}, bf16[272,512]{1,0:T(8,128)(2,1)S(1)}, u32[]{:S(2)}, u32[]{:S(2)}) collective-permute-start(bf16[272,512]{1,0:T(8,128)(2,1)S(1)} %add_select_fusion.refs_0_), channel_id=1, source_target_pairs={{0,1},{1,0},{2,3},{3,2},{4,5},{5,4},{6,7},{7,6},{8,9},{9,8},{10,11... | collective-permute-start | bytes 835592 | tf_op jit(solution)/shard_map/ppermute | solution.py:347
  40.1 20.7 %collective-permute-start.11 = (bf16[272,512]{1,0:T(8,128)(2,1)S(1)}, bf16[272,512]{1,0:T(8,128)(2,1)S(1)}, u32[]{:S(2)}, u32[]{:S(2)}) collective-permute-start(bf16[272,512]{1,0:T(8,128)(2,1)S(1)} %collective-permute-done.7.refs_1_), channel_id=1, source_target_pairs={{0,1},{1,0},{2,3},{3,2},{4,5},{5,4},{6,7},{7,6},{8,9},{9,8},{10,11... | collective-permute-start | bytes 835592 | tf_op jit(solution)/shard_map/ppermute | solution.py:347
  41.7 19.1 %collective-permute-start.12 = (bf16[272,512]{1,0:T(8,128)(2,1)S(1)}, bf16[272,512]{1,0:T(8,128)(2,1)S(1)}, u32[]{:S(2)}, u32[]{:S(2)}) collective-permute-start(bf16[272,512]{1,0:T(8,128)(2,1)S(1)} %collective-permute-done.8.refs_2_), channel_id=1, source_target_pairs={{0,1},{1,0},{2,3},{3,2},{4,5},{5,4},{6,7},{7,6},{8,9},{9,8},{10,11... | collective-permute-start | bytes 835592 | tf_op jit(solution)/shard_map/ppermute | solution.py:347
  44.4 16.4 %collective-permute-start.13 = (bf16[272,512]{1,0:T(8,128)(2,1)S(1)}, bf16[272,512]{1,0:T(8,128)(2,1)S(1)}, u32[]{:S(2)}, u32[]{:S(2)}) collective-permute-start(bf16[272,512]{1,0:T(8,128)(2,1)S(1)} %collective-permute-done.9.refs_3_), channel_id=1, source_target_pairs={{0,1},{1,0},{2,3},{3,2},{4,5},{5,4},{6,7},{7,6},{8,9},{9,8},{10,11... | collective-permute-start | bytes 835592 | tf_op jit(solution)/shard_map/ppermute | solution.py:347
  95.2 27.9 %all-to-all-start.1 = ((f32[32,16,512]{2,1,0:T(8,128)}), f32[32,16,512]{2,1,0:T(8,128)S(1)}, u32[]{:S(2)}, u32[]{:S(2)}) async-start(f32[32,16,512]{2,1,0:T(8,128)} %broadcast_in_dim.13), calls=%async_computation.1 | async-start | bytes 2097152 | tf_op jit(solution)/shard_map/all_to_all | solution.py:412
  106.0 73.9 %all-reduce.3.cloned.1.call-start = ((), (), s32[]{:S(2)}) async-start(), calls=%async_computation.2 | async-start | bytes 3145728 | tf_op jit(solution)/shard_map/psum | solution.py:410
  150.3 0.8 copy-start
  151.1 0.8 copy-start.1
Sparse Core Ops, SparseCore 0:
  109.2 70.7 all-reduce.2
